TPU v7x, 512 devices: a whole 4x8x8 slice. The times are simulated.
512 devices in a mesh: blk: 128 (over z, y, core), tok: 4 (over x).
Axes of the slice: x: 4, y: 8, z: 8, core: 2. Of those that a mesh axis runs over, the one named last changes fastest.
Arguments:
- queries: bfloat16 [4096, 32, 128], P('blk'), may hold values from -0.5 to 0.5
- candidates: int32 [4096, 4], P('blk'), may hold values from 0 to 127, all different within a row; in each aligned block of 32 rows (0 to 31, 32 to 63, ...) at most 2 rows name the same one
- passages: bfloat16 [128, 180, 32, 128], P('blk', 'tok'), may hold values from -0.5 to 0.5
- lengths: int32 [128, 32], P('blk'), may hold values from 1 to 180
Outputs:
- maxsim: float32 [4096, 4, 32], P('blk', None, 'tok')
Inputs may be any that keep to these rules, and one draw needn't show every extreme that they name: `candidates`: each row names 4 different blocks. Among the rows of one index of blk no block is named more than 2 times, and in every draw some block is named exactly 2 times by the rows of some index.
All inputs are finite; a program needn't handle non-finite values.
Results may differ from a plain program's by a relative error of at most 0.0003.
Values may be sent and summed in bfloat16 or wider, within the bound.
No kernel may reach another device: no remote copies, remote signals or barrier semaphores. Data moves between devices by JAX's collectives and lax.ppermute only.
A program may use at most 64 MiB of HBM per device.

v0:
```python
import functools
import itertools
import math

import jax
import jax.numpy as jnp
from jax import lax
from jax.experimental import pallas as pl
from jax.experimental.pallas import tpu as pltpu
from jax.sharding import PartitionSpec as P


CORES = 2
FLAG = 2.0
VMEM = pl.BlockSpec(memory_space=pltpu.VMEM)
SMEM = pl.BlockSpec(memory_space=pltpu.SMEM)
LANES = 128


def build_kernel(cand_ref, query_ref, out_ref, table, *, turn):
    pair_k, pair_q = cand_ref.shape
    owners = table.shape[0]
    core = lax.axis_index("blk") % CORES
    plane = lax.axis_index("tok")
    owner_core = core ^ (plane // 2)
    backward = plane % 2 == 0
    pairs = pair_k * pair_q
    for d in range(owners):
        table[d] = 0
    for i in range(pairs):
        p = jnp.where(backward, pairs - 1 - i, i)
        table[cand_ref[p // pair_q, p % pair_q]] = p % pair_q
    chips = owners // CORES
    for place in range(chips):
        chip = (place + turn) % chips
        out_ref[place] = query_ref[table[chip * CORES + owner_core]]


def score_kernel(*refs, tile, piece, query_len):
    *part_refs, query_ref, out_ref, token_ref = refs
    slots_len, width, dim = token_ref.shape
    length = part_refs[0].shape[0]
    items = tile // query_len
    plane = lax.axis_index("tok")
    first = part_refs[0][0]
    for shift in range(1, len(part_refs)):
        first = jnp.where(plane == shift, part_refs[shift][0], first)
    for shift, part_ref in enumerate(part_refs):
        for j in range(length):
            token = part_ref[j]
            token_ref[shift * length + j] = jnp.where(token > 1, first, token)

    def one_tile(index, carry):
        rows = query_ref[pl.ds(pl.multiple_of(index * tile, tile), tile), :]
        best = None
        for start in range(0, slots_len, piece):
            segment = token_ref[start : start + piece].reshape(piece * width, dim)
            scores = lax.dot_general(
                segment, rows, (((1,), (1,)), ((), ())), preferred_element_type=jnp.float32
            )
            top = jnp.max(scores.reshape(piece, width, tile), axis=0)
            best = top if best is None else jnp.maximum(best, top)
        flipped = jnp.transpose(best).reshape(items, query_len, width)
        out_ref[pl.ds(pl.multiple_of(index * items, items), items), :] = jnp.sum(flipped, axis=1)
        return carry

    lax.fori_loop(0, query_ref.shape[0] // tile, one_tile, 0)


def turn_kernel(in_ref, out_ref):
    parts, part_width, _ = out_ref.shape
    slots = in_ref.shape[0]
    flipped = jnp.transpose(in_ref[...])
    flipped = jnp.concatenate([flipped] * (LANES // slots), axis=1)
    for part in range(parts):
        out_ref[part] = flipped[part * part_width : (part + 1) * part_width]


def pick_kernel(in_ref, lane_ref, plane_ref, out_ref):
    planes, part_width, _ = in_ref.shape
    cand_count, _, query_count = out_ref.shape
    lanes = jnp.broadcast_to(lane_ref[...], (part_width, LANES))
    which = jnp.broadcast_to(plane_ref[...], (part_width, LANES))
    picked = None
    for plane in range(planes):
        got = jnp.take_along_axis(in_ref[plane], lanes, axis=1)
        picked = got if picked is None else jnp.where(which == plane, got, picked)
    for k in range(cand_count):
        out_ref[k] = picked[:, k * query_count : (k + 1) * query_count]


def near(*arrays):
    return [pltpu.with_memory_space_constraint(array, pltpu.VMEM) for array in arrays]


def make_groups(mesh):
    owners = mesh.shape["blk"]
    parts = mesh.shape["tok"]
    chips = owners // CORES
    turn = chips // 2 + math.isqrt(chips) // 2
    across = [[(place + turn) % chips * CORES + core for place in range(chips)] for core in range(CORES)]
    routes = []
    for shift in range(parts):
        pairs = []
        for blk, part in itertools.product(range(owners), range(parts)):
            plane = (part + shift) % parts
            pairs.append((blk * parts + part, (blk ^ (plane // 2)) * parts + plane))
        routes.append(pairs)
    return dict(across=across, routes=routes, turn=turn)


def shards(queries, candidates, passages, lengths, *, across, routes, turn):
    num_owners = lax.axis_size("blk")
    num_parts = lax.axis_size("tok")
    part_idx = lax.axis_index("tok")
    core = lax.axis_index("blk") % CORES
    query_count, query_len, dim_width = queries.shape
    cand_count = candidates.shape[1]
    local_len = passages.shape[1]
    pass_width = passages.shape[2]
    part_width = pass_width // num_parts
    chips = num_owners // CORES

    turned = candidates.T
    outgoing = pl.pallas_call(
        functools.partial(build_kernel, turn=turn),
        out_shape=pltpu.VMEM((chips, query_len, dim_width), queries.dtype),
        in_specs=[SMEM, VMEM],
        out_specs=VMEM,
        scratch_shapes=[pltpu.SMEM((num_owners,), jnp.int32)],
        name="build",
    )(turned, queries)
    received = lax.all_to_all(
        outgoing, "blk", split_axis=0, concat_axis=0, axis_index_groups=across, tiled=True
    )

    token_pos = part_idx * local_len + jnp.arange(local_len, dtype=jnp.int32)
    valid = token_pos[:, None] < lengths[0][None, :]
    flagged = jnp.where(valid[..., None], passages[0], jnp.array(FLAG, passages.dtype))
    parts = []
    for pairs in routes:
        parts.append(lax.ppermute(flagged, ("blk", "tok"), pairs))

    named = turned.reshape(cand_count * query_count)
    order = jnp.arange(cand_count * query_count, dtype=jnp.int32)
    earlier = (named[:, None] == named[None, :]) & (order[:, None] < order[None, :])
    position = jnp.sum(earlier.astype(jnp.int32), axis=0)
    lane = ((named // CORES - turn) % chips).reshape(1, -1)
    plane = (((named % CORES) ^ core) * 2 + position).reshape(1, -1)
    received, lane, plane = lax.optimization_barrier((received, lane, plane))
    totals = pl.pallas_call(
        lambda *refs: score_kernel(*refs, tile=512, piece=60, query_len=query_len),
        out_shape=pltpu.VMEM((chips, pass_width), jnp.float32),
        in_specs=[VMEM] * (num_parts + 1),
        out_specs=VMEM,
        scratch_shapes=[pltpu.VMEM((num_parts * local_len, pass_width, dim_width), passages.dtype)],
        name="score",
    )(*near(*parts, received.reshape(chips * query_len, dim_width)))

    returned = lax.all_to_all(
        totals.reshape(chips, 1, pass_width), "blk", split_axis=0, concat_axis=0,
        axis_index_groups=across, tiled=True,
    ).reshape(chips, pass_width)
    spread = pl.pallas_call(
        turn_kernel,
        out_shape=pltpu.VMEM((num_parts, part_width, LANES), jnp.float32),
        in_specs=[VMEM],
        out_specs=VMEM,
        name="turn",
    )(*near(returned))
    gathered = lax.all_to_all(spread, "tok", split_axis=0, concat_axis=0, tiled=True)

    picked = pl.pallas_call(
        pick_kernel,
        out_shape=jax.ShapeDtypeStruct((cand_count, part_width, query_count), jnp.float32),
        in_specs=[VMEM, VMEM, VMEM],
        out_specs=VMEM,
        name="pick",
    )(*near(gathered, lane, plane))
    return jnp.transpose(picked, (2, 0, 1))


def solution(mesh):
    in_specs = (P("blk", None, None), P("blk", None), P("blk", "tok", None, None), P("blk", None))
    out_specs = P("blk", None, "tok")
    groups = make_groups(mesh)

    def local(*args):
        return shards(*args, **groups)

    return jax.shard_map(local, mesh=mesh, in_specs=in_specs, out_specs=out_specs, check_vma=False)
```

profile of v0, /device:TPU:1, one launch (start us, length us, event | category | flops | bytes accessed | tf_op | source)
XLA Modules:
  0.0 80.9 jit_solution(6901487567654389183)
XLA Ops:
  0.0 2.6 %build.1 = bf16[64,32,128]{2,1,0:T(8,128)(2,1)} custom-call(s32[4,32]{1,0:T(4,128)} %bitcast.15, bf16[32,32,128]{2,1,0:T(8,128)(2,1)} %query_ref.1), custom_call_target="tpu_custom_call" | custom-call | tf_op jit(solution)/shard_map/build/pallas_call | solution.py:125
  2.6 0.0 copy-start
  2.6 20.2 %all-to-all-start = ((bf16[64,32,128]{2,1,0:T(8,128)(2,1)}), bf16[64,32,128]{2,1,0:T(8,128)(2,1)S(1)}, u32[]{:S(2)}, u32[]{:S(2)}) async-start(bf16[64,32,128]{2,1,0:T(8,128)(2,1)} %build.1), calls=%async_computation | async-start | bytes 1048576 | tf_op jit(solution)/shard_map/all_to_all | solution.py:133
  22.8 0.0 copy-start.2
  22.8 0.6 copy-done.2
  23.5 0.1 broadcast_compare_fusion
  23.5 0.0 copy-done
  23.5 0.3 bitcast_select_fusion
  23.8 0.7 collective-permute-start
  24.5 3.1 %collective-permute-start.1 = (bf16[45,32,128]{2,1,0:T(8,128)(2,1)S(1)}, bf16[45,32,128]{2,1,0:T(8,128)(2,1)S(1)}, u32[]{:S(2)}, u32[]{:S(2)}) collective-permute-start(bf16[45,32,128]{2,1,0:T(8,128)(2,1)S(1)} %bitcast_select_fusion), channel_id=1, source_target_pairs={{0,1},{1,6},{2,7},{3,0},{4,5},{5,2},{6,3},{7,4},{8,9},{9,14},{10,1... | collective-permute-start | bytes 1105928 | tf_op jit(solution)/shard_map/ppermute | solution.py:142
  27.6 7.1 %collective-permute-start.2 = (bf16[45,32,128]{2,1,0:T(8,128)(2,1)S(1)}, bf16[45,32,128]{2,1,0:T(8,128)(2,1)S(1)}, u32[]{:S(2)}, u32[]{:S(2)}) collective-permute-start(bf16[45,32,128]{2,1,0:T(8,128)(2,1)S(1)} %bitcast_select_fusion), channel_id=1, source_target_pairs={{0,6},{1,7},{2,0},{3,1},{4,2},{5,3},{6,4},{7,5},{8,14},{9,15},{10,... | collective-permute-start | bytes 1105928 | tf_op jit(solution)/shard_map/ppermute | solution.py:142
  34.7 3.3 %collective-permute-start.3 = (bf16[45,32,128]{2,1,0:T(8,128)(2,1)S(1)}, bf16[45,32,128]{2,1,0:T(8,128)(2,1)S(1)}, u32[]{:S(2)}, u32[]{:S(2)}) collective-permute-start(bf16[45,32,128]{2,1,0:T(8,128)(2,1)S(1)} %bitcast_select_fusion), channel_id=1, source_target_pairs={{0,7},{1,0},{2,1},{3,6},{4,3},{5,4},{6,5},{7,2},{8,15},{9,8},{10,9... | collective-permute-start | bytes 1105928 | tf_op jit(solution)/shard_map/ppermute | solution.py:142
  38.1 0.0 copy-start.1
  38.1 0.7 copy-done.1
  38.8 0.1 eq.20
  38.8 0.1 reshape.199
  38.9 0.1 convert_reduce_fusion
  39.1 0.0 all-to-all-done
  39.1 0.0 collective-permute-done.refs_0_
  39.1 1.2 %collective-permute-done.1.refs_1_ = bf16[45,32,128]{2,1,0:T(8,128)(2,1)S(1)} collective-permute-done((bf16[45,32,128]{2,1,0:T(8,128)(2,1)S(1)}, bf16[45,32,128]{2,1,0:T(8,128)(2,1)S(1)}, u32[]{:S(2)}, u32[]{:S(2)}) %collective-permute-start.1) | collective-permute-done | bytes 368672 | tf_op jit(solution)/shard_map/ppermute | solution.py:142
  40.3 8.5 %collective-permute-done.2.refs_2_ = bf16[45,32,128]{2,1,0:T(8,128)(2,1)S(1)} collective-permute-done((bf16[45,32,128]{2,1,0:T(8,128)(2,1)S(1)}, bf16[45,32,128]{2,1,0:T(8,128)(2,1)S(1)}, u32[]{:S(2)}, u32[]{:S(2)}) %collective-permute-start.2) | collective-permute-done | bytes 368672 | tf_op jit(solution)/shard_map/ppermute | solution.py:142
  48.8 1.4 %collective-permute-done.3.refs_3_ = bf16[45,32,128]{2,1,0:T(8,128)(2,1)S(1)} collective-permute-done((bf16[45,32,128]{2,1,0:T(8,128)(2,1)S(1)}, bf16[45,32,128]{2,1,0:T(8,128)(2,1)S(1)}, u32[]{:S(2)}, u32[]{:S(2)}) %collective-permute-start.3) | collective-permute-done | bytes 368672 | tf_op jit(solution)/shard_map/ppermute | solution.py:142
  50.1 7.7 %score.1 = f32[64,32]{1,0:T(8,128)S(1)} custom-call(bf16[45,32,128]{2,1,0:T(8,128)(2,1)S(1)} %collective-permute-done.refs_0_, bf16[45,32,128]{2,1,0:T(8,128)(2,1)S(1)} %collective-permute-done.1.refs_1_, bf16[45,32,128]{2,1,0:T(8,128)(2,1)S(1)} %collective-permute-done.2.refs_2_, bf16[45,32,128]{2,1,0:T(8,128)(2,1)S(1)} %collective-permute-done.3.refs_3_, ...), custom_call_target="tpu_custom_call" | custom-call | tf_op jit(solution)/shard_map/score/pallas_call | solution.py:151
  57.9 13.5 %all_to_all.15 = f32[64,1,32]{2,1,0:T(1,128)S(1)} all-to-all(f32[64,1,32]{2,1,0:T(1,128)S(1)} %bitcast.13), channel_id=1, replica_groups={{288,296,304,312,320,328,336,344,352,360,368,376,384,392,400,408,416,42..., dimensions={0} | all-to-all | bytes 16384 | tf_op jit(solution)/shard_map/all_to_all | solution.py:160
  71.4 0.1 turn.1
  71.5 8.6 %all_to_all.16.in_ref = f32[4,8,128]{2,1,0:T(8,128)S(1)} all-to-all(f32[4,8,128]{2,1,0:T(8,128)S(1)} %turn.1), channel_id=1, replica_groups=mesh['blk'=128,'tok'=4] {'tok'}, dimensions={0} | all-to-all | bytes 32768 | tf_op jit(solution)/shard_map/all_to_all | solution.py:171
  80.2 0.8 pick.1
  (2 shorter events, 0.0 us)
Async XLA Ops:
  2.6 21.0 %copy-start = (bf16[1,45,32,128]{3,2,1,0:T(8,128)(2,1)S(1)}, bf16[1,45,32,128]{3,2,1,0:T(8,128)(2,1)}, u32[]{:S(2)}) copy-start(bf16[1,45,32,128]{3,2,1,0:T(8,128)(2,1)} %param.6) | copy-start | bytes 1105924
  2.6 36.5 %all-to-all-start = ((bf16[64,32,128]{2,1,0:T(8,128)(2,1)}), bf16[64,32,128]{2,1,0:T(8,128)(2,1)S(1)}, u32[]{:S(2)}, u32[]{:S(2)}) async-start(bf16[64,32,128]{2,1,0:T(8,128)(2,1)} %build.1), calls=%async_computation | async-start | bytes 1048576 | tf_op jit(solution)/shard_map/all_to_all | solution.py:133
  22.8 0.7 copy-start.2
  23.8 15.3 %collective-permute-start = (bf16[45,32,128]{2,1,0:T(8,128)(2,1)S(1)}, bf16[45,32,128]{2,1,0:T(8,128)(2,1)S(1)}, u32[]{:S(2)}, u32[]{:S(2)}) collective-permute-start(bf16[45,32,128]{2,1,0:T(8,128)(2,1)S(1)} %bitcast_select_fusion), channel_id=1, source_target_pairs={{0,0},{1,1},{2,6},{3,7},{4,4},{5,5},{6,2},{7,3},{8,8},{9,9},{10,14... | collective-permute-start | bytes 1105928 | tf_op jit(solution)/shard_map/ppermute | solution.py:142
  24.5 15.8 %collective-permute-start.1 = (bf16[45,32,128]{2,1,0:T(8,128)(2,1)S(1)}, bf16[45,32,128]{2,1,0:T(8,128)(2,1)S(1)}, u32[]{:S(2)}, u32[]{:S(2)}) collective-permute-start(bf16[45,32,128]{2,1,0:T(8,128)(2,1)S(1)} %bitcast_select_fusion), channel_id=1, source_target_pairs={{0,1},{1,6},{2,7},{3,0},{4,5},{5,2},{6,3},{7,4},{8,9},{9,14},{10,1... | collective-permute-start | bytes 1105928 | tf_op jit(solution)/shard_map/ppermute | solution.py:142
  27.6 21.1 %collective-permute-start.2 = (bf16[45,32,128]{2,1,0:T(8,128)(2,1)S(1)}, bf16[45,32,128]{2,1,0:T(8,128)(2,1)S(1)}, u32[]{:S(2)}, u32[]{:S(2)}) collective-permute-start(bf16[45,32,128]{2,1,0:T(8,128)(2,1)S(1)} %bitcast_select_fusion), channel_id=1, source_target_pairs={{0,6},{1,7},{2,0},{3,1},{4,2},{5,3},{6,4},{7,5},{8,14},{9,15},{10,... | collective-permute-start | bytes 1105928 | tf_op jit(solution)/shard_map/ppermute | solution.py:142
  34.7 15.4 %collective-permute-start.3 = (bf16[45,32,128]{2,1,0:T(8,128)(2,1)S(1)}, bf16[45,32,128]{2,1,0:T(8,128)(2,1)S(1)}, u32[]{:S(2)}, u32[]{:S(2)}) collective-permute-start(bf16[45,32,128]{2,1,0:T(8,128)(2,1)S(1)} %bitcast_select_fusion), channel_id=1, source_target_pairs={{0,7},{1,0},{2,1},{3,6},{4,3},{5,4},{6,5},{7,2},{8,15},{9,8},{10,9... | collective-permute-start | bytes 1105928 | tf_op jit(solution)/shard_map/ppermute | solution.py:142
  38.1 0.7 copy-start.1
where the time goes:
time: 82.6 us; the launch traced here: 80.9 us
  starting transfers between devices  34.4 us (42%)
  blocking collectives  22.2 us (27%)
  Pallas kernels  11.2 us (14%)
  waiting for transfers between devices  11.1 us (13%)
  local copies, waits for them, and re-layouts  1.49 us (2%)
    all_to_all x1, starting transfers between devices, shards(): lax.all_to_all(outgoing, 'blk', split_axis=0, concat_axis=0, axis_index_g...  20.2 us
    ppermute x4, starting transfers between devices, shards(): parts.append(lax.ppermute(flagged, ('blk', 'tok'), pairs))  14.2 us
    all_to_all x1, blocking collectives, shards(): lax.all_to_all(totals.reshape(chips, 1, pass_width), 'blk', split_axis=0,...  13.5 us
    ppermute x4, waiting for transfers between devices, shards(): parts.append(lax.ppermute(flagged, ('blk', 'tok'), pairs))  11.1 us
    all_to_all x1, blocking collectives, shards(): lax.all_to_all(spread, 'tok', split_axis=0, concat_axis=0, tiled=True)  8.63 us
    pallas_call x1, Pallas kernels, shards(): pl.pallas_call(lambda *refs: score_kernel(*refs, tile=512, piece=60, quer...  7.73 us
    pallas_call x1, Pallas kernels, shards(): pl.pallas_call(functools.partial(build_kernel, turn=turn), out_shape=pltp...  2.57 us
  transfers between devices with their start and end apart: 5, of which 3 were waited for; matrix products, arithmetic and copies ran while one was open for 1% of the time, Pallas kernels for 0%

commit v1 on v0

--- a/solution.py
+++ b/solution.py
@@ -11,57 +11,74 @@
 
 
 CORES = 2
-FLAG = 2.0
 VMEM = pl.BlockSpec(memory_space=pltpu.VMEM)
 SMEM = pl.BlockSpec(memory_space=pltpu.SMEM)
 LANES = 128
-
-
-def build_kernel(cand_ref, query_ref, out_ref, table, *, turn):
+TILE = 512
+FIRST, SECOND = (0, 2), (1, 3)
+NEGATIVE_FILL = -1e30
+
+
+def build_kernel(cand_ref, query_hbm, out_ref, table, query_ref, sem, *, turn):
+    fetch = pltpu.make_async_copy(query_hbm, query_ref, sem)
+    fetch.start()
     pair_k, pair_q = cand_ref.shape
     owners = table.shape[0]
-    core = lax.axis_index("blk") % CORES
+    chips = owners // CORES
     plane = lax.axis_index("tok")
-    owner_core = core ^ (plane // 2)
-    backward = plane % 2 == 0
-    pairs = pair_k * pair_q
-    for d in range(owners):
-        table[d] = 0
-    for i in range(pairs):
-        p = jnp.where(backward, pairs - 1 - i, i)
-        table[cand_ref[p // pair_q, p % pair_q]] = p % pair_q
-    chips = owners // CORES
+    owner_core = lax.axis_index("blk") % CORES ^ (plane // 2)
+    pairs = [(k, q) for k in range(pair_k) for q in range(pair_q)]
+    for chip in range(chips):
+        table[chip * CORES + owner_core] = 0
+
+    @pl.when(plane % 2 == 0)
+    def _():
+        for k, q in reversed(pairs):
+            table[cand_ref[k, q]] = q
+
+    @pl.when(plane % 2 == 1)
+    def _():
+        for k, q in pairs:
+            table[cand_ref[k, q]] = q
+
+    fetch.wait()
     for place in range(chips):
         chip = (place + turn) % chips
         out_ref[place] = query_ref[table[chip * CORES + owner_core]]
 
 
-def score_kernel(*refs, tile, piece, query_len):
-    *part_refs, query_ref, out_ref, token_ref = refs
-    slots_len, width, dim = token_ref.shape
-    length = part_refs[0].shape[0]
+def best_kernel(*refs, shifts, parts, tile, query_len, last):
+    *given_refs, ends_ref, query_ref, out_ref, token_ref = refs
+    part_refs, before_refs = given_refs[: len(shifts)], given_refs[len(shifts) :]
+    length, width, dim = token_ref.shape[1:]
     items = tile // query_len
     plane = lax.axis_index("tok")
-    first = part_refs[0][0]
-    for shift in range(1, len(part_refs)):
-        first = jnp.where(plane == shift, part_refs[shift][0], first)
-    for shift, part_ref in enumerate(part_refs):
+    ends = ends_ref[0].astype(jnp.float32)
+    used = []
+    for place, shift in enumerate(shifts):
+        start = ((plane - shift + parts) % parts * length).astype(jnp.float32)
+        used.append(jnp.concatenate([ends > start] * (tile // LANES), axis=1))
+        left = (ends - start).astype(token_ref.dtype)
+        first = part_refs[place][0]
         for j in range(length):
-            token = part_ref[j]
-            token_ref[shift * length + j] = jnp.where(token > 1, first, token)
+            token_ref[place, j] = jnp.where(left > j, part_refs[place][j], first)
 
     def one_tile(index, carry):
         rows = query_ref[pl.ds(pl.multiple_of(index * tile, tile), tile), :]
-        best = None
-        for start in range(0, slots_len, piece):
-            segment = token_ref[start : start + piece].reshape(piece * width, dim)
+        best = before_refs[0][index] if before_refs else None
+        for place in range(len(shifts)):
             scores = lax.dot_general(
-                segment, rows, (((1,), (1,)), ((), ())), preferred_element_type=jnp.float32
+                token_ref[place].reshape(length * width, dim), rows, (((1,), (1,)), ((), ())),
+                preferred_element_type=jnp.float32,
             )
-            top = jnp.max(scores.reshape(piece, width, tile), axis=0)
+            top = jnp.max(scores.reshape(length, width, tile), axis=0)
+            top = jnp.where(used[place], top, NEGATIVE_FILL)
             best = top if best is None else jnp.maximum(best, top)
-        flipped = jnp.transpose(best).reshape(items, query_len, width)
-        out_ref[pl.ds(pl.multiple_of(index * items, items), items), :] = jnp.sum(flipped, axis=1)
+        if last:
+            flipped = jnp.transpose(best).reshape(items, query_len, width)
+            out_ref[pl.ds(pl.multiple_of(index * items, items), items), :] = jnp.sum(flipped, axis=1)
+        else:
+            out_ref[index] = best
         return carry
 
     lax.fori_loop(0, query_ref.shape[0] // tile, one_tile, 0)
@@ -112,7 +129,6 @@
 def shards(queries, candidates, passages, lengths, *, across, routes, turn):
     num_owners = lax.axis_size("blk")
     num_parts = lax.axis_size("tok")
-    part_idx = lax.axis_index("tok")
     core = lax.axis_index("blk") % CORES
     query_count, query_len, dim_width = queries.shape
     cand_count = candidates.shape[1]
@@ -122,24 +138,29 @@
     chips = num_owners // CORES
 
     turned = candidates.T
-    outgoing = pl.pallas_call(
+    build = pl.pallas_call(
         functools.partial(build_kernel, turn=turn),
         out_shape=pltpu.VMEM((chips, query_len, dim_width), queries.dtype),
-        in_specs=[SMEM, VMEM],
+        in_specs=[SMEM, pl.BlockSpec(memory_space=pl.ANY)],
         out_specs=VMEM,
-        scratch_shapes=[pltpu.SMEM((num_owners,), jnp.int32)],
+        scratch_shapes=[
+            pltpu.SMEM((num_owners,), jnp.int32),
+            pltpu.VMEM(queries.shape, queries.dtype),
+            pltpu.SemaphoreType.DMA,
+        ],
         name="build",
-    )(turned, queries)
+    )
+    outgoing = build(turned, queries)
     received = lax.all_to_all(
         outgoing, "blk", split_axis=0, concat_axis=0, axis_index_groups=across, tiled=True
     )
 
-    token_pos = part_idx * local_len + jnp.arange(local_len, dtype=jnp.int32)
-    valid = token_pos[:, None] < lengths[0][None, :]
-    flagged = jnp.where(valid[..., None], passages[0], jnp.array(FLAG, passages.dtype))
+    own = passages[0]
+    ends = jnp.broadcast_to(lengths[0][None, :, None], (1, pass_width, dim_width)).astype(own.dtype)
     parts = []
-    for pairs in routes:
-        parts.append(lax.ppermute(flagged, ("blk", "tok"), pairs))
+    for shift, pairs in enumerate(routes):
+        payload = own if shift else jnp.concatenate([own, ends])
+        parts.append(lax.ppermute(payload, ("blk", "tok"), pairs))
 
     named = turned.reshape(cand_count * query_count)
     order = jnp.arange(cand_count * query_count, dtype=jnp.int32)
@@ -148,14 +169,25 @@
     lane = ((named // CORES - turn) % chips).reshape(1, -1)
     plane = (((named % CORES) ^ core) * 2 + position).reshape(1, -1)
     received, lane, plane = lax.optimization_barrier((received, lane, plane))
-    totals = pl.pallas_call(
-        lambda *refs: score_kernel(*refs, tile=512, piece=60, query_len=query_len),
-        out_shape=pltpu.VMEM((chips, pass_width), jnp.float32),
-        in_specs=[VMEM] * (num_parts + 1),
-        out_specs=VMEM,
-        scratch_shapes=[pltpu.VMEM((num_parts * local_len, pass_width, dim_width), passages.dtype)],
-        name="score",
-    )(*near(*parts, received.reshape(chips * query_len, dim_width)))
+    rows = received.reshape(chips * query_len, dim_width)
+    ends = parts[0][local_len:]
+    maxima = None
+    for shifts in FIRST, SECOND:
+        last = shifts is SECOND
+        whole = (chips, pass_width) if last else (rows.shape[0] // TILE, pass_width, TILE)
+        kernel = functools.partial(
+            best_kernel, shifts=shifts, parts=num_parts, tile=TILE, query_len=query_len, last=last
+        )
+        inputs = [parts[shift] for shift in shifts] + ([maxima] if last else []) + [ends, rows]
+        maxima = pl.pallas_call(
+            kernel,
+            out_shape=pltpu.VMEM(whole, jnp.float32),
+            in_specs=[VMEM] * len(inputs),
+            out_specs=VMEM,
+            scratch_shapes=[pltpu.VMEM((len(shifts), local_len, pass_width, dim_width), own.dtype)],
+            name="best",
+        )(*near(*inputs))
+    totals = maxima
 
     returned = lax.all_to_all(
         totals.reshape(chips, 1, pass_width), "blk", split_axis=0, concat_axis=0,

time: 82.6 us -> 76.6 us (0.927)
  the two profiles are of different devices: /device:TPU:1 before, /device:TPU:8 now
where the time goes in v1:
time: 76.6 us; the launch traced here: 76.2 us
  starting transfers between devices  32.3 us (42%)
  blocking collectives  25.1 us (33%)
  Pallas kernels  11.7 us (15%)
  waiting for transfers between devices  5.94 us (8%)
  local copies, waits for them, and re-layouts  0.93 us (1%)
    all_to_all x1, starting transfers between devices, shards(): lax.all_to_all(outgoing, 'blk', split_axis=0, concat_axis=0, axis_index_g...  18.9 us
    all_to_all x1, blocking collectives, shards(): lax.all_to_all(totals.reshape(chips, 1, pass_width), 'blk', split_axis=0,...  15.8 us
    ppermute x4, starting transfers between devices, shards(): parts.append(lax.ppermute(payload, ('blk', 'tok'), pairs))  13.3 us
    all_to_all x1, blocking collectives, shards(): lax.all_to_all(spread, 'tok', split_axis=0, concat_axis=0, tiled=True)  9.31 us
    pallas_call x2, Pallas kernels, shards(): pl.pallas_call(kernel, out_shape=pltpu.VMEM(whole, jnp.float32), in_specs...  8.28 us
    ppermute x4, waiting for transfers between devices, shards(): parts.append(lax.ppermute(payload, ('blk', 'tok'), pairs))  5.94 us
    pallas_call x1, Pallas kernels, shards(): outgoing = build(turned, queries)  2.49 us
  transfers between devices with their start and end apart: 5, of which 3 were waited for; matrix products, arithmetic and copies ran while one was open for 1% of the time, Pallas kernels for 5%

profile of v1, /device:TPU:8, one launch (start us, length us, event | category | flops | bytes accessed | tf_op | source)
XLA Modules:
  0.0 76.2 jit_solution(5354259185346284986)
XLA Ops:
  0.0 2.5 %build.1 = bf16[64,32,128]{2,1,0:T(8,128)(2,1)} custom-call(s32[4,32]{1,0:T(4,128)} %bitcast.20, bf16[32,32,128]{2,1,0:T(8,128)(2,1)} %query_hbm.1), custom_call_target="tpu_custom_call" | custom-call | tf_op jit(solution)/shard_map/build/pallas_call | solution.py:153
  2.5 0.0 copy-start.2
  2.5 0.0 copy-start
  2.5 18.9 %all-to-all-start = ((bf16[64,32,128]{2,1,0:T(8,128)(2,1)}), bf16[64,32,128]{2,1,0:T(8,128)(2,1)S(1)}, u32[]{:S(2)}, u32[]{:S(2)}) async-start(bf16[64,32,128]{2,1,0:T(8,128)(2,1)} %build.1), calls=%async_computation | async-start | bytes 1048576 | tf_op jit(solution)/shard_map/all_to_all | solution.py:154
  21.5 0.0 copy-done.2
  21.5 0.1 broadcast_in_dim.2
  21.6 0.0 copy-done
  21.6 0.7 collective-permute-start.2
  22.3 6.3 %collective-permute-start.3 = (bf16[45,32,128]{2,1,0:T(8,128)(2,1)S(1)}, bf16[45,32,128]{2,1,0:T(8,128)(2,1)S(1)}, u32[]{:S(2)}, u32[]{:S(2)}) collective-permute-start(bf16[45,32,128]{2,1,0:T(8,128)(2,1)S(1)} %bitcast.17), channel_id=1, source_target_pairs={{0,6},{1,7},{2,0},{3,1},{4,2},{5,3},{6,4},{7,5},{8,14},{9,15},{10,... | collective-permute-start | bytes 1105928 | tf_op jit(solution)/shard_map/ppermute | solution.py:163
  28.6 2.5 %collective-permute-start = (bf16[45,32,128]{2,1,0:T(8,128)(2,1)S(1)}, bf16[45,32,128]{2,1,0:T(8,128)(2,1)S(1)}, u32[]{:S(2)}, u32[]{:S(2)}) collective-permute-start(bf16[45,32,128]{2,1,0:T(8,128)(2,1)S(1)} %bitcast.18), channel_id=1, source_target_pairs={{0,1},{1,6},{2,7},{3,0},{4,5},{5,2},{6,3},{7,4},{8,9},{9,14},{10,1... | collective-permute-start | bytes 1105928 | tf_op jit(solution)/shard_map/ppermute | solution.py:163
  31.1 3.9 %collective-permute-start.1 = (bf16[45,32,128]{2,1,0:T(8,128)(2,1)S(1)}, bf16[45,32,128]{2,1,0:T(8,128)(2,1)S(1)}, u32[]{:S(2)}, u32[]{:S(2)}) collective-permute-start(bf16[45,32,128]{2,1,0:T(8,128)(2,1)S(1)} %bitcast.19), channel_id=1, source_target_pairs={{0,7},{1,0},{2,1},{3,6},{4,3},{5,4},{6,5},{7,2},{8,15},{9,8},{10,9... | collective-permute-start | bytes 1105928 | tf_op jit(solution)/shard_map/ppermute | solution.py:163
  35.0 0.0 copy-start.1
  35.0 0.7 copy-done.1
  35.7 0.1 eq.20
  35.8 0.1 reshape.172
  35.8 0.1 convert_reduce_fusion
  36.0 0.0 collective-permute-done.2.refs_0_
  36.0 0.0 all-to-all-done
  36.0 1.9 %collective-permute-done.3.refs_1_ = bf16[45,32,128]{2,1,0:T(8,128)(2,1)S(1)} collective-permute-done((bf16[45,32,128]{2,1,0:T(8,128)(2,1)S(1)}, bf16[45,32,128]{2,1,0:T(8,128)(2,1)S(1)}, u32[]{:S(2)}, u32[]{:S(2)}) %collective-permute-start.3) | collective-permute-done | bytes 368672 | tf_op jit(solution)/shard_map/ppermute | solution.py:163
  38.0 3.9 %best.2.refs_2_ = f32[4,32,512]{2,1,0:T(8,128)S(1)} custom-call(bf16[46,32,128]{2,1,0:T(8,128)(2,1)S(1)} %collective-permute-done.2.refs_0_, bf16[45,32,128]{2,1,0:T(8,128)(2,1)S(1)} %collective-permute-done.3.refs_1_, bf16[1,32,128]{2,1,0:T(8,128)(2,1)S(1)} %slice.4.refs_2_.refs_3_, bf16[2048,128]{1,0:T(8,128)(2,1)S(1)} %bitcast.12), custom_call_target="tpu_custom_call" | custom-call | tf_op jit(solution)/shard_map/best/pallas_call | solution.py:182
  41.8 3.8 %collective-permute-done.refs_0_ = bf16[45,32,128]{2,1,0:T(8,128)(2,1)S(1)} collective-permute-done((bf16[45,32,128]{2,1,0:T(8,128)(2,1)S(1)}, bf16[45,32,128]{2,1,0:T(8,128)(2,1)S(1)}, u32[]{:S(2)}, u32[]{:S(2)}) %collective-permute-start) | collective-permute-done | bytes 368672 | tf_op jit(solution)/shard_map/ppermute | solution.py:163
  45.6 0.2 collective-permute-done.1.refs_1_
  45.8 4.4 %best.3 = f32[64,32]{1,0:T(8,128)S(1)} custom-call(bf16[45,32,128]{2,1,0:T(8,128)(2,1)S(1)} %collective-permute-done.refs_0_, bf16[45,32,128]{2,1,0:T(8,128)(2,1)S(1)} %collective-permute-done.1.refs_1_, f32[4,32,512]{2,1,0:T(8,128)S(1)} %best.2.refs_2_, bf16[1,32,128]{2,1,0:T(8,128)(2,1)S(1)} %slice.4.refs_2_.refs_3_, bf16[2048,128]{1,0:T(8,128)(2,1)S(1)} %bitcast.13), custom_call_target="tpu_custom_call" | custom-call | tf_op jit(solution)/shard_map/best/pallas_call | solution.py:182
  50.2 15.8 %all_to_all.15 = f32[64,1,32]{2,1,0:T(1,128)S(1)} all-to-all(f32[64,1,32]{2,1,0:T(1,128)S(1)} %bitcast.14), channel_id=1, replica_groups={{288,296,304,312,320,328,336,344,352,360,368,376,384,392,400,408,416,42..., dimensions={0} | all-to-all | bytes 16384 | tf_op jit(solution)/shard_map/all_to_all | solution.py:192
  66.0 0.1 turn.1
  66.1 9.3 %all_to_all.16.in_ref = f32[4,8,128]{2,1,0:T(8,128)S(1)} all-to-all(f32[4,8,128]{2,1,0:T(8,128)S(1)} %turn.1), channel_id=1, replica_groups=mesh['blk'=128,'tok'=4] {'tok'}, dimensions={0} | all-to-all | bytes 32768 | tf_op jit(solution)/shard_map/all_to_all | solution.py:203
  75.4 0.8 pick.1
  (4 shorter events, 0.1 us)
Async XLA Ops:
  2.5 19.0 %copy-start.2 = (s32[1,32]{1,0:T(1,128)S(1)}, s32[1,32]{1,0:T(1,128)}, u32[]{:S(2)}) copy-start(s32[1,32]{1,0:T(1,128)} %param.7) | copy-start | bytes 388
  2.5 19.1 %copy-start = (bf16[1,45,32,128]{3,2,1,0:T(8,128)(2,1)S(1)}, bf16[1,45,32,128]{3,2,1,0:T(8,128)(2,1)}, u32[]{:S(2)}) copy-start(bf16[1,45,32,128]{3,2,1,0:T(8,128)(2,1)} %param.6) | copy-start | bytes 1105924
  2.5 33.5 %all-to-all-start = ((bf16[64,32,128]{2,1,0:T(8,128)(2,1)}), bf16[64,32,128]{2,1,0:T(8,128)(2,1)S(1)}, u32[]{:S(2)}, u32[]{:S(2)}) async-start(bf16[64,32,128]{2,1,0:T(8,128)(2,1)} %build.1), calls=%async_computation | async-start | bytes 1048576 | tf_op jit(solution)/shard_map/all_to_all | solution.py:154
  21.6 14.4 %collective-permute-start.2 = (bf16[46,32,128]{2,1,0:T(8,128)(2,1)S(1)}, bf16[46,32,128]{2,1,0:T(8,128)(2,1)S(1)}, u32[]{:S(2)}, u32[]{:S(2)}) collective-permute-start(bf16[46,32,128]{2,1,0:T(8,128)(2,1)S(1)} %pad_maximum_fusion), channel_id=1, source_target_pairs={{0,0},{1,1},{2,6},{3,7},{4,4},{5,5},{6,2},{7,3},{8,8},{9,9},{10,14... | collective-permute-start | bytes 1130504 | tf_op jit(solution)/shard_map/ppermute | solution.py:163
  22.3 15.6 %collective-permute-start.3 = (bf16[45,32,128]{2,1,0:T(8,128)(2,1)S(1)}, bf16[45,32,128]{2,1,0:T(8,128)(2,1)S(1)}, u32[]{:S(2)}, u32[]{:S(2)}) collective-permute-start(bf16[45,32,128]{2,1,0:T(8,128)(2,1)S(1)} %bitcast.17), channel_id=1, source_target_pairs={{0,6},{1,7},{2,0},{3,1},{4,2},{5,3},{6,4},{7,5},{8,14},{9,15},{10,... | collective-permute-start | bytes 1105928 | tf_op jit(solution)/shard_map/ppermute | solution.py:163
  28.6 17.0 %collective-permute-start = (bf16[45,32,128]{2,1,0:T(8,128)(2,1)S(1)}, bf16[45,32,128]{2,1,0:T(8,128)(2,1)S(1)}, u32[]{:S(2)}, u32[]{:S(2)}) collective-permute-start(bf16[45,32,128]{2,1,0:T(8,128)(2,1)S(1)} %bitcast.18), channel_id=1, source_target_pairs={{0,1},{1,6},{2,7},{3,0},{4,5},{5,2},{6,3},{7,4},{8,9},{9,14},{10,1... | collective-permute-start | bytes 1105928 | tf_op jit(solution)/shard_map/ppermute | solution.py:163
  31.1 14.7 %collective-permute-start.1 = (bf16[45,32,128]{2,1,0:T(8,128)(2,1)S(1)}, bf16[45,32,128]{2,1,0:T(8,128)(2,1)S(1)}, u32[]{:S(2)}, u32[]{:S(2)}) collective-permute-start(bf16[45,32,128]{2,1,0:T(8,128)(2,1)S(1)} %bitcast.19), channel_id=1, source_target_pairs={{0,7},{1,0},{2,1},{3,6},{4,3},{5,4},{6,5},{7,2},{8,15},{9,8},{10,9... | collective-permute-start | bytes 1105928 | tf_op jit(solution)/shard_map/ppermute | solution.py:163
  35.0 0.7 copy-start.1

commit v2 on v1

--- a/solution.py
+++ b/solution.py
@@ -19,8 +19,10 @@
 NEGATIVE_FILL = -1e30
 
 
-def build_kernel(cand_ref, query_hbm, out_ref, table, query_ref, sem, *, turn):
-    fetch = pltpu.make_async_copy(query_hbm, query_ref, sem)
+def build_kernel(cand_hbm, query_hbm, out_ref, table, cand_ref, query_ref, sems, *, turn):
+    named = pltpu.make_async_copy(cand_hbm, cand_ref, sems.at[0])
+    fetch = pltpu.make_async_copy(query_hbm, query_ref, sems.at[1])
+    named.start()
     fetch.start()
     pair_k, pair_q = cand_ref.shape
     owners = table.shape[0]
@@ -30,6 +32,7 @@
     pairs = [(k, q) for k in range(pair_k) for q in range(pair_q)]
     for chip in range(chips):
         table[chip * CORES + owner_core] = 0
+    named.wait()
 
     @pl.when(plane % 2 == 0)
     def _():
@@ -47,7 +50,7 @@
         out_ref[place] = query_ref[table[chip * CORES + owner_core]]
 
 
-def best_kernel(*refs, shifts, parts, tile, query_len, last):
+def best_kernel(*refs, shifts, parts, tile, query_len, delta, last):
     *given_refs, ends_ref, query_ref, out_ref, token_ref = refs
     part_refs, before_refs = given_refs[: len(shifts)], given_refs[len(shifts) :]
     length, width, dim = token_ref.shape[1:]
@@ -76,7 +79,8 @@
             best = top if best is None else jnp.maximum(best, top)
         if last:
             flipped = jnp.transpose(best).reshape(items, query_len, width)
-            out_ref[pl.ds(pl.multiple_of(index * items, items), items), :] = jnp.sum(flipped, axis=1)
+            row = (index * items + delta) % out_ref.shape[0]
+            out_ref[pl.ds(pl.multiple_of(row, items), items), :] = jnp.sum(flipped, axis=1)
         else:
             out_ref[index] = best
         return carry
@@ -114,8 +118,12 @@
     owners = mesh.shape["blk"]
     parts = mesh.shape["tok"]
     chips = owners // CORES
-    turn = chips // 2 + math.isqrt(chips) // 2
-    across = [[(place + turn) % chips * CORES + core for place in range(chips)] for core in range(CORES)]
+    turn = chips // 2 + chips // 8 + math.isqrt(chips) // 2
+    back = turn
+
+    def same_core(start):
+        return [[(place + start) % chips * CORES + core for place in range(chips)] for core in range(CORES)]
+
     routes = []
     for shift in range(parts):
         pairs = []
@@ -123,10 +131,10 @@
             plane = (part + shift) % parts
             pairs.append((blk * parts + part, (blk ^ (plane // 2)) * parts + plane))
         routes.append(pairs)
-    return dict(across=across, routes=routes, turn=turn)
-
-
-def shards(queries, candidates, passages, lengths, *, across, routes, turn):
+    return dict(across=same_core(turn), homeward=same_core(back), routes=routes, turn=turn, back=back)
+
+
+def shards(queries, candidates, passages, lengths, *, across, homeward, routes, turn, back):
     num_owners = lax.axis_size("blk")
     num_parts = lax.axis_size("tok")
     core = lax.axis_index("blk") % CORES
@@ -141,12 +149,13 @@
     build = pl.pallas_call(
         functools.partial(build_kernel, turn=turn),
         out_shape=pltpu.VMEM((chips, query_len, dim_width), queries.dtype),
-        in_specs=[SMEM, pl.BlockSpec(memory_space=pl.ANY)],
+        in_specs=[pl.BlockSpec(memory_space=pl.ANY)] * 2,
         out_specs=VMEM,
         scratch_shapes=[
             pltpu.SMEM((num_owners,), jnp.int32),
+            pltpu.SMEM(turned.shape, turned.dtype),
             pltpu.VMEM(queries.shape, queries.dtype),
-            pltpu.SemaphoreType.DMA,
+            pltpu.SemaphoreType.DMA((2,)),
         ],
         name="build",
     )
@@ -166,7 +175,7 @@
     order = jnp.arange(cand_count * query_count, dtype=jnp.int32)
     earlier = (named[:, None] == named[None, :]) & (order[:, None] < order[None, :])
     position = jnp.sum(earlier.astype(jnp.int32), axis=0)
-    lane = ((named // CORES - turn) % chips).reshape(1, -1)
+    lane = ((named // CORES - back) % chips).reshape(1, -1)
     plane = (((named % CORES) ^ core) * 2 + position).reshape(1, -1)
     received, lane, plane = lax.optimization_barrier((received, lane, plane))
     rows = received.reshape(chips * query_len, dim_width)
@@ -176,7 +185,8 @@
         last = shifts is SECOND
         whole = (chips, pass_width) if last else (rows.shape[0] // TILE, pass_width, TILE)
         kernel = functools.partial(
-            best_kernel, shifts=shifts, parts=num_parts, tile=TILE, query_len=query_len, last=last
+            best_kernel, shifts=shifts, parts=num_parts, tile=TILE, query_len=query_len,
+            delta=(turn - back) % chips, last=last
         )
         inputs = [parts[shift] for shift in shifts] + ([maxima] if last else []) + [ends, rows]
         maxima = pl.pallas_call(
@@ -191,7 +201,7 @@
 
     returned = lax.all_to_all(
         totals.reshape(chips, 1, pass_width), "blk", split_axis=0, concat_axis=0,
-        axis_index_groups=across, tiled=True,
+        axis_index_groups=homeward, tiled=True,
     ).reshape(chips, pass_width)
     spread = pl.pallas_call(
         turn_kernel,

time: 76.6 us -> 75.9 us (level)
  starting transfers between devices: 32.3 us -> 31.3 us
  blocking collectives: 25.1 us -> 26 us
    all_to_all x1, starting transfers between devices: 18.9 us -> 18 us  [shards(): lax.all_to_all(outgoing, 'blk', split_axis=0, concat_axis=0, axis_index_g...]
    all_to_all x1, blocking collectives: 15.8 us -> 16.7 us  [shards(): lax.all_to_all(totals.reshape(chips, 1, pass_width), 'blk', split_axis=0,...]
where the time goes in v2:
time: 75.9 us; the launch traced here: 75.5 us
  starting transfers between devices  31.3 us (41%)
  blocking collectives  26 us (34%)
  Pallas kernels  11 us (14%)
  waiting for transfers between devices  5.94 us (8%)
  local copies, waits for them, and re-layouts  0.93 us (1%)
    all_to_all x1, starting transfers between devices, shards(): lax.all_to_all(outgoing, 'blk', split_axis=0, concat_axis=0, axis_index_g...  18 us
    all_to_all x1, blocking collectives, shards(): lax.all_to_all(totals.reshape(chips, 1, pass_width), 'blk', split_axis=0,...  16.7 us
    ppermute x4, starting transfers between devices, shards(): parts.append(lax.ppermute(payload, ('blk', 'tok'), pairs))  13.3 us
    all_to_all x1, blocking collectives, shards(): lax.all_to_all(spread, 'tok', split_axis=0, concat_axis=0, tiled=True)  9.31 us
    pallas_call x2, Pallas kernels, shards(): pl.pallas_call(kernel, out_shape=pltpu.VMEM(whole, jnp.float32), in_specs...  8.28 us
    ppermute x4, waiting for transfers between devices, shards(): parts.append(lax.ppermute(payload, ('blk', 'tok'), pairs))  5.94 us
    pallas_call x1, Pallas kernels, shards(): outgoing = build(turned, queries)  1.81 us
  transfers between devices with their start and end apart: 5, of which 3 were waited for; matrix products, arithmetic and copies ran while one was open for 1% of the time, Pallas kernels for 5%

profile of v2, /device:TPU:8, one launch (start us, length us, event | category | flops | bytes accessed | tf_op | source)
XLA Modules:
  0.0 75.5 jit_solution(9966174855175796817)
XLA Ops:
  0.0 1.8 %build.1 = bf16[64,32,128]{2,1,0:T(8,128)(2,1)} custom-call(s32[4,32]{1,0:T(4,128)} %bitcast.20, bf16[32,32,128]{2,1,0:T(8,128)(2,1)} %query_hbm.1), custom_call_target="tpu_custom_call" | custom-call | tf_op jit(solution)/shard_map/build/pallas_call | solution.py:162
  1.8 0.0 copy-start.2
  1.8 0.0 copy-start
  1.8 18.0 %all-to-all-start = ((bf16[64,32,128]{2,1,0:T(8,128)(2,1)}), bf16[64,32,128]{2,1,0:T(8,128)(2,1)S(1)}, u32[]{:S(2)}, u32[]{:S(2)}) async-start(bf16[64,32,128]{2,1,0:T(8,128)(2,1)} %build.1), calls=%async_computation | async-start | bytes 1048576 | tf_op jit(solution)/shard_map/all_to_all | solution.py:163
  19.8 0.0 copy-done.2
  19.9 0.1 broadcast_in_dim.2
  19.9 0.0 copy-done
  20.0 0.7 collective-permute-start.2
  20.7 6.3 %collective-permute-start.3 = (bf16[45,32,128]{2,1,0:T(8,128)(2,1)S(1)}, bf16[45,32,128]{2,1,0:T(8,128)(2,1)S(1)}, u32[]{:S(2)}, u32[]{:S(2)}) collective-permute-start(bf16[45,32,128]{2,1,0:T(8,128)(2,1)S(1)} %bitcast.17), channel_id=1, source_target_pairs={{0,6},{1,7},{2,0},{3,1},{4,2},{5,3},{6,4},{7,5},{8,14},{9,15},{10,... | collective-permute-start | bytes 1105928 | tf_op jit(solution)/shard_map/ppermute | solution.py:172
  26.9 2.5 %collective-permute-start = (bf16[45,32,128]{2,1,0:T(8,128)(2,1)S(1)}, bf16[45,32,128]{2,1,0:T(8,128)(2,1)S(1)}, u32[]{:S(2)}, u32[]{:S(2)}) collective-permute-start(bf16[45,32,128]{2,1,0:T(8,128)(2,1)S(1)} %bitcast.18), channel_id=1, source_target_pairs={{0,1},{1,6},{2,7},{3,0},{4,5},{5,2},{6,3},{7,4},{8,9},{9,14},{10,1... | collective-permute-start | bytes 1105928 | tf_op jit(solution)/shard_map/ppermute | solution.py:172
  29.5 3.9 %collective-permute-start.1 = (bf16[45,32,128]{2,1,0:T(8,128)(2,1)S(1)}, bf16[45,32,128]{2,1,0:T(8,128)(2,1)S(1)}, u32[]{:S(2)}, u32[]{:S(2)}) collective-permute-start(bf16[45,32,128]{2,1,0:T(8,128)(2,1)S(1)} %bitcast.19), channel_id=1, source_target_pairs={{0,7},{1,0},{2,1},{3,6},{4,3},{5,4},{6,5},{7,2},{8,15},{9,8},{10,9... | collective-permute-start | bytes 1105928 | tf_op jit(solution)/shard_map/ppermute | solution.py:172
  33.4 0.0 copy-start.1
  33.4 0.7 copy-done.1
  34.0 0.1 eq.20
  34.1 0.1 reshape.172
  34.2 0.1 convert_reduce_fusion
  34.3 0.0 collective-permute-done.2.refs_0_
  34.4 0.0 all-to-all-done
  34.4 1.9 %collective-permute-done.3.refs_1_ = bf16[45,32,128]{2,1,0:T(8,128)(2,1)S(1)} collective-permute-done((bf16[45,32,128]{2,1,0:T(8,128)(2,1)S(1)}, bf16[45,32,128]{2,1,0:T(8,128)(2,1)S(1)}, u32[]{:S(2)}, u32[]{:S(2)}) %collective-permute-start.3) | collective-permute-done | bytes 368672 | tf_op jit(solution)/shard_map/ppermute | solution.py:172
  36.3 3.9 %best.2.refs_2_ = f32[4,32,512]{2,1,0:T(8,128)S(1)} custom-call(bf16[46,32,128]{2,1,0:T(8,128)(2,1)S(1)} %collective-permute-done.2.refs_0_, bf16[45,32,128]{2,1,0:T(8,128)(2,1)S(1)} %collective-permute-done.3.refs_1_, bf16[1,32,128]{2,1,0:T(8,128)(2,1)S(1)} %slice.4.refs_2_.refs_3_, bf16[2048,128]{1,0:T(8,128)(2,1)S(1)} %bitcast.12), custom_call_target="tpu_custom_call" | custom-call | tf_op jit(solution)/shard_map/best/pallas_call | solution.py:192
  40.2 3.8 %collective-permute-done.refs_0_ = bf16[45,32,128]{2,1,0:T(8,128)(2,1)S(1)} collective-permute-done((bf16[45,32,128]{2,1,0:T(8,128)(2,1)S(1)}, bf16[45,32,128]{2,1,0:T(8,128)(2,1)S(1)}, u32[]{:S(2)}, u32[]{:S(2)}) %collective-permute-start) | collective-permute-done | bytes 368672 | tf_op jit(solution)/shard_map/ppermute | solution.py:172
  44.0 0.2 collective-permute-done.1.refs_1_
  44.2 4.4 %best.3 = f32[64,32]{1,0:T(8,128)S(1)} custom-call(bf16[45,32,128]{2,1,0:T(8,128)(2,1)S(1)} %collective-permute-done.refs_0_, bf16[45,32,128]{2,1,0:T(8,128)(2,1)S(1)} %collective-permute-done.1.refs_1_, f32[4,32,512]{2,1,0:T(8,128)S(1)} %best.2.refs_2_, bf16[1,32,128]{2,1,0:T(8,128)(2,1)S(1)} %slice.4.refs_2_.refs_3_, bf16[2048,128]{1,0:T(8,128)(2,1)S(1)} %bitcast.13), custom_call_target="tpu_custom_call" | custom-call | tf_op jit(solution)/shard_map/best/pallas_call | solution.py:192
  48.6 16.7 %all_to_all.15 = f32[64,1,32]{2,1,0:T(1,128)S(1)} all-to-all(f32[64,1,32]{2,1,0:T(1,128)S(1)} %bitcast.14), channel_id=1, replica_groups={{352,360,368,376,384,392,400,408,416,424,432,440,448,456,464,472,480,48..., dimensions={0} | all-to-all | bytes 16384 | tf_op jit(solution)/shard_map/all_to_all | solution.py:202
  65.3 0.1 turn.1
  65.4 9.3 %all_to_all.16.in_ref = f32[4,8,128]{2,1,0:T(8,128)S(1)} all-to-all(f32[4,8,128]{2,1,0:T(8,128)S(1)} %turn.1), channel_id=1, replica_groups=mesh['blk'=128,'tok'=4] {'tok'}, dimensions={0} | all-to-all | bytes 32768 | tf_op jit(solution)/shard_map/all_to_all | solution.py:213
  74.7 0.8 pick.1
  (4 shorter events, 0.1 us)
Async XLA Ops:
  1.8 18.0 %copy-start.2 = (s32[1,32]{1,0:T(1,128)S(1)}, s32[1,32]{1,0:T(1,128)}, u32[]{:S(2)}) copy-start(s32[1,32]{1,0:T(1,128)} %param.7) | copy-start | bytes 388
  1.8 18.1 %copy-start = (bf16[1,45,32,128]{3,2,1,0:T(8,128)(2,1)S(1)}, bf16[1,45,32,128]{3,2,1,0:T(8,128)(2,1)}, u32[]{:S(2)}) copy-start(bf16[1,45,32,128]{3,2,1,0:T(8,128)(2,1)} %param.6) | copy-start | bytes 1105924
  1.8 32.5 %all-to-all-start = ((bf16[64,32,128]{2,1,0:T(8,128)(2,1)}), bf16[64,32,128]{2,1,0:T(8,128)(2,1)S(1)}, u32[]{:S(2)}, u32[]{:S(2)}) async-start(bf16[64,32,128]{2,1,0:T(8,128)(2,1)} %build.1), calls=%async_computation | async-start | bytes 1048576 | tf_op jit(solution)/shard_map/all_to_all | solution.py:163
  20.0 14.4 %collective-permute-start.2 = (bf16[46,32,128]{2,1,0:T(8,128)(2,1)S(1)}, bf16[46,32,128]{2,1,0:T(8,128)(2,1)S(1)}, u32[]{:S(2)}, u32[]{:S(2)}) collective-permute-start(bf16[46,32,128]{2,1,0:T(8,128)(2,1)S(1)} %pad_maximum_fusion), channel_id=1, source_target_pairs={{0,0},{1,1},{2,6},{3,7},{4,4},{5,5},{6,2},{7,3},{8,8},{9,9},{10,14... | collective-permute-start | bytes 1130504 | tf_op jit(solution)/shard_map/ppermute | solution.py:172
  20.7 15.6 %collective-permute-start.3 = (bf16[45,32,128]{2,1,0:T(8,128)(2,1)S(1)}, bf16[45,32,128]{2,1,0:T(8,128)(2,1)S(1)}, u32[]{:S(2)}, u32[]{:S(2)}) collective-permute-start(bf16[45,32,128]{2,1,0:T(8,128)(2,1)S(1)} %bitcast.17), channel_id=1, source_target_pairs={{0,6},{1,7},{2,0},{3,1},{4,2},{5,3},{6,4},{7,5},{8,14},{9,15},{10,... | collective-permute-start | bytes 1105928 | tf_op jit(solution)/shard_map/ppermute | solution.py:172
  26.9 17.0 %collective-permute-start = (bf16[45,32,128]{2,1,0:T(8,128)(2,1)S(1)}, bf16[45,32,128]{2,1,0:T(8,128)(2,1)S(1)}, u32[]{:S(2)}, u32[]{:S(2)}) collective-permute-start(bf16[45,32,128]{2,1,0:T(8,128)(2,1)S(1)} %bitcast.18), channel_id=1, source_target_pairs={{0,1},{1,6},{2,7},{3,0},{4,5},{5,2},{6,3},{7,4},{8,9},{9,14},{10,1... | collective-permute-start | bytes 1105928 | tf_op jit(solution)/shard_map/ppermute | solution.py:172
  29.5 14.7 %collective-permute-start.1 = (bf16[45,32,128]{2,1,0:T(8,128)(2,1)S(1)}, bf16[45,32,128]{2,1,0:T(8,128)(2,1)S(1)}, u32[]{:S(2)}, u32[]{:S(2)}) collective-permute-start(bf16[45,32,128]{2,1,0:T(8,128)(2,1)S(1)} %bitcast.19), channel_id=1, source_target_pairs={{0,7},{1,0},{2,1},{3,6},{4,3},{5,4},{6,5},{7,2},{8,15},{9,8},{10,9... | collective-permute-start | bytes 1105928 | tf_op jit(solution)/shard_map/ppermute | solution.py:172
  33.4 0.7 copy-start.1

commit v3 on v1

--- a/solution.py
+++ b/solution.py
@@ -14,13 +14,15 @@
 VMEM = pl.BlockSpec(memory_space=pltpu.VMEM)
 SMEM = pl.BlockSpec(memory_space=pltpu.SMEM)
 LANES = 128
-TILE = 512
+TILE = 2048
 FIRST, SECOND = (0, 2), (1, 3)
 NEGATIVE_FILL = -1e30
 
 
-def build_kernel(cand_ref, query_hbm, out_ref, table, query_ref, sem, *, turn):
-    fetch = pltpu.make_async_copy(query_hbm, query_ref, sem)
+def build_kernel(cand_hbm, query_hbm, out_ref, table, cand_ref, query_ref, sems, *, turn):
+    named = pltpu.make_async_copy(cand_hbm, cand_ref, sems.at[0])
+    fetch = pltpu.make_async_copy(query_hbm, query_ref, sems.at[1])
+    named.start()
     fetch.start()
     pair_k, pair_q = cand_ref.shape
     owners = table.shape[0]
@@ -30,6 +32,7 @@
     pairs = [(k, q) for k in range(pair_k) for q in range(pair_q)]
     for chip in range(chips):
         table[chip * CORES + owner_core] = 0
+    named.wait()
 
     @pl.when(plane % 2 == 0)
     def _():
@@ -114,7 +117,7 @@
     owners = mesh.shape["blk"]
     parts = mesh.shape["tok"]
     chips = owners // CORES
-    turn = chips // 2 + math.isqrt(chips) // 2
+    turn = chips // 2 + chips // 8 + math.isqrt(chips) // 2
     across = [[(place + turn) % chips * CORES + core for place in range(chips)] for core in range(CORES)]
     routes = []
     for shift in range(parts):
@@ -141,12 +144,13 @@
     build = pl.pallas_call(
         functools.partial(build_kernel, turn=turn),
         out_shape=pltpu.VMEM((chips, query_len, dim_width), queries.dtype),
-        in_specs=[SMEM, pl.BlockSpec(memory_space=pl.ANY)],
+        in_specs=[pl.BlockSpec(memory_space=pl.ANY)] * 2,
         out_specs=VMEM,
         scratch_shapes=[
             pltpu.SMEM((num_owners,), jnp.int32),
+            pltpu.SMEM(turned.shape, turned.dtype),
             pltpu.VMEM(queries.shape, queries.dtype),
-            pltpu.SemaphoreType.DMA,
+            pltpu.SemaphoreType.DMA((2,)),
         ],
         name="build",
     )

time: 76.6 us -> 74.9 us (0.978)
  Pallas kernels: 11.7 us -> 9.35 us
  starting transfers between devices: 32.3 us -> 31.3 us
  blocking collectives: 25.1 us -> 26 us
    pallas_call x2, Pallas kernels: 8.28 us -> 6.66 us  [shards(): pl.pallas_call(kernel, out_shape=pltpu.VMEM(whole, jnp.float32), in_specs...]
    all_to_all x1, starting transfers between devices: 18.9 us -> 18 us  [shards(): lax.all_to_all(outgoing, 'blk', split_axis=0, concat_axis=0, axis_index_g...]
    all_to_all x1, blocking collectives: 15.8 us -> 16.7 us  [shards(): lax.all_to_all(totals.reshape(chips, 1, pass_width), 'blk', split_axis=0,...]
  transfers between devices with their start and end apart: 5 -> 5, of which waited for: 3 -> 3; matrix products, arithmetic and copies ran while one was open for 1% -> 1% of each run, Pallas kernels for 5% -> 4%
where the time goes in v3:
time: 74.9 us; the launch traced here: 74.5 us
  starting transfers between devices  31.3 us (42%)
  blocking collectives  26 us (35%)
  Pallas kernels  9.35 us (12%)
  waiting for transfers between devices  6.56 us (9%)
  local copies, waits for them, and re-layouts  0.93 us (1%)
    all_to_all x1, starting transfers between devices, shards(): lax.all_to_all(outgoing, 'blk', split_axis=0, concat_axis=0, axis_index_g...  18 us
    all_to_all x1, blocking collectives, shards(): lax.all_to_all(totals.reshape(chips, 1, pass_width), 'blk', split_axis=0,...  16.7 us
    ppermute x4, starting transfers between devices, shards(): parts.append(lax.ppermute(payload, ('blk', 'tok'), pairs))  13.3 us
    all_to_all x1, blocking collectives, shards(): lax.all_to_all(spread, 'tok', split_axis=0, concat_axis=0, tiled=True)  9.31 us
    pallas_call x2, Pallas kernels, shards(): pl.pallas_call(kernel, out_shape=pltpu.VMEM(whole, jnp.float32), in_specs...  6.66 us
    ppermute x4, waiting for transfers between devices, shards(): parts.append(lax.ppermute(payload, ('blk', 'tok'), pairs))  6.56 us
    pallas_call x1, Pallas kernels, shards(): outgoing = build(turned, queries)  1.81 us
  transfers between devices with their start and end apart: 5, of which 3 were waited for; matrix products, arithmetic and copies ran while one was open for 1% of the time, Pallas kernels for 4%

profile of v3, /device:TPU:8, one launch (start us, length us, event | category | flops | bytes accessed | tf_op | source)
XLA Modules:
  0.0 74.5 jit_solution(1630478020854745826)
XLA Ops:
  0.0 1.8 %build.1 = bf16[64,32,128]{2,1,0:T(8,128)(2,1)} custom-call(s32[4,32]{1,0:T(4,128)} %bitcast.20, bf16[32,32,128]{2,1,0:T(8,128)(2,1)} %query_hbm.1), custom_call_target="tpu_custom_call" | custom-call | tf_op jit(solution)/shard_map/build/pallas_call | solution.py:157
  1.8 0.0 copy-start.2
  1.8 0.0 copy-start
  1.8 18.0 %all-to-all-start = ((bf16[64,32,128]{2,1,0:T(8,128)(2,1)}), bf16[64,32,128]{2,1,0:T(8,128)(2,1)S(1)}, u32[]{:S(2)}, u32[]{:S(2)}) async-start(bf16[64,32,128]{2,1,0:T(8,128)(2,1)} %build.1), calls=%async_computation | async-start | bytes 1048576 | tf_op jit(solution)/shard_map/all_to_all | solution.py:158
  19.8 0.0 copy-done.2
  19.9 0.1 broadcast_in_dim.2
  19.9 0.0 copy-done
  20.0 0.7 collective-permute-start.2
  20.7 6.3 %collective-permute-start.3 = (bf16[45,32,128]{2,1,0:T(8,128)(2,1)S(1)}, bf16[45,32,128]{2,1,0:T(8,128)(2,1)S(1)}, u32[]{:S(2)}, u32[]{:S(2)}) collective-permute-start(bf16[45,32,128]{2,1,0:T(8,128)(2,1)S(1)} %bitcast.17), channel_id=1, source_target_pairs={{0,6},{1,7},{2,0},{3,1},{4,2},{5,3},{6,4},{7,5},{8,14},{9,15},{10,... | collective-permute-start | bytes 1105928 | tf_op jit(solution)/shard_map/ppermute | solution.py:167
  26.9 2.5 %collective-permute-start = (bf16[45,32,128]{2,1,0:T(8,128)(2,1)S(1)}, bf16[45,32,128]{2,1,0:T(8,128)(2,1)S(1)}, u32[]{:S(2)}, u32[]{:S(2)}) collective-permute-start(bf16[45,32,128]{2,1,0:T(8,128)(2,1)S(1)} %bitcast.18), channel_id=1, source_target_pairs={{0,1},{1,6},{2,7},{3,0},{4,5},{5,2},{6,3},{7,4},{8,9},{9,14},{10,1... | collective-permute-start | bytes 1105928 | tf_op jit(solution)/shard_map/ppermute | solution.py:167
  29.5 3.9 %collective-permute-start.1 = (bf16[45,32,128]{2,1,0:T(8,128)(2,1)S(1)}, bf16[45,32,128]{2,1,0:T(8,128)(2,1)S(1)}, u32[]{:S(2)}, u32[]{:S(2)}) collective-permute-start(bf16[45,32,128]{2,1,0:T(8,128)(2,1)S(1)} %bitcast.19), channel_id=1, source_target_pairs={{0,7},{1,0},{2,1},{3,6},{4,3},{5,4},{6,5},{7,2},{8,15},{9,8},{10,9... | collective-permute-start | bytes 1105928 | tf_op jit(solution)/shard_map/ppermute | solution.py:167
  33.4 0.0 copy-start.1
  33.4 0.7 copy-done.1
  34.0 0.1 eq.20
  34.1 0.1 reshape.172
  34.2 0.1 convert_reduce_fusion
  34.3 0.0 collective-permute-done.2.refs_0_
  34.4 0.0 all-to-all-done
  34.4 1.9 %collective-permute-done.3.refs_1_ = bf16[45,32,128]{2,1,0:T(8,128)(2,1)S(1)} collective-permute-done((bf16[45,32,128]{2,1,0:T(8,128)(2,1)S(1)}, bf16[45,32,128]{2,1,0:T(8,128)(2,1)S(1)}, u32[]{:S(2)}, u32[]{:S(2)}) %collective-permute-start.3) | collective-permute-done | bytes 368672 | tf_op jit(solution)/shard_map/ppermute | solution.py:167
  36.3 3.2 %best.2.refs_2_ = f32[1,32,2048]{2,1,0:T(8,128)S(1)} custom-call(bf16[46,32,128]{2,1,0:T(8,128)(2,1)S(1)} %collective-permute-done.2.refs_0_, bf16[45,32,128]{2,1,0:T(8,128)(2,1)S(1)} %collective-permute-done.3.refs_1_, bf16[1,32,128]{2,1,0:T(8,128)(2,1)S(1)} %slice.4.refs_2_.refs_3_, bf16[2048,128]{1,0:T(8,128)(2,1)S(1)} %bitcast.12), custom_call_target="tpu_custom_call" | custom-call | tf_op jit(solution)/shard_map/best/pallas_call | solution.py:186
  39.6 4.4 %collective-permute-done.refs_0_ = bf16[45,32,128]{2,1,0:T(8,128)(2,1)S(1)} collective-permute-done((bf16[45,32,128]{2,1,0:T(8,128)(2,1)S(1)}, bf16[45,32,128]{2,1,0:T(8,128)(2,1)S(1)}, u32[]{:S(2)}, u32[]{:S(2)}) %collective-permute-start) | collective-permute-done | bytes 368672 | tf_op jit(solution)/shard_map/ppermute | solution.py:167
  44.0 0.2 collective-permute-done.1.refs_1_
  44.2 3.4 %best.3 = f32[64,32]{1,0:T(8,128)S(1)} custom-call(bf16[45,32,128]{2,1,0:T(8,128)(2,1)S(1)} %collective-permute-done.refs_0_, bf16[45,32,128]{2,1,0:T(8,128)(2,1)S(1)} %collective-permute-done.1.refs_1_, f32[1,32,2048]{2,1,0:T(8,128)S(1)} %best.2.refs_2_, bf16[1,32,128]{2,1,0:T(8,128)(2,1)S(1)} %slice.4.refs_2_.refs_3_, bf16[2048,128]{1,0:T(8,128)(2,1)S(1)} %bitcast.13), custom_call_target="tpu_custom_call" | custom-call | tf_op jit(solution)/shard_map/best/pallas_call | solution.py:186
  47.6 16.7 %all_to_all.15 = f32[64,1,32]{2,1,0:T(1,128)S(1)} all-to-all(f32[64,1,32]{2,1,0:T(1,128)S(1)} %bitcast.14), channel_id=1, replica_groups={{352,360,368,376,384,392,400,408,416,424,432,440,448,456,464,472,480,48..., dimensions={0} | all-to-all | bytes 16384 | tf_op jit(solution)/shard_map/all_to_all | solution.py:196
  64.3 0.1 turn.1
  64.4 9.3 %all_to_all.16.in_ref = f32[4,8,128]{2,1,0:T(8,128)S(1)} all-to-all(f32[4,8,128]{2,1,0:T(8,128)S(1)} %turn.1), channel_id=1, replica_groups=mesh['blk'=128,'tok'=4] {'tok'}, dimensions={0} | all-to-all | bytes 32768 | tf_op jit(solution)/shard_map/all_to_all | solution.py:207
  73.7 0.8 %pick.1 = f32[4,8,32]{2,1,0:T(8,128)} custom-call(f32[4,8,128]{2,1,0:T(8,128)S(1)} %all_to_all.16.in_ref, s32[1,128]{1,0:T(1,128)S(1)} %get-tuple-element.9.lane_ref, s32[1,128]{1,0:T(1,128)S(1)} %get-tuple-element.10.plane_ref), custom_call_target="tpu_custom_call" | custom-call | tf_op jit(solution)/shard_map/pick/pallas_call | solution.py:209
  (4 shorter events, 0.1 us)
Async XLA Ops:
  1.8 18.0 %copy-start.2 = (s32[1,32]{1,0:T(1,128)S(1)}, s32[1,32]{1,0:T(1,128)}, u32[]{:S(2)}) copy-start(s32[1,32]{1,0:T(1,128)} %param.7) | copy-start | bytes 388
  1.8 18.1 %copy-start = (bf16[1,45,32,128]{3,2,1,0:T(8,128)(2,1)S(1)}, bf16[1,45,32,128]{3,2,1,0:T(8,128)(2,1)}, u32[]{:S(2)}) copy-start(bf16[1,45,32,128]{3,2,1,0:T(8,128)(2,1)} %param.6) | copy-start | bytes 1105924
  1.8 32.5 %all-to-all-start = ((bf16[64,32,128]{2,1,0:T(8,128)(2,1)}), bf16[64,32,128]{2,1,0:T(8,128)(2,1)S(1)}, u32[]{:S(2)}, u32[]{:S(2)}) async-start(bf16[64,32,128]{2,1,0:T(8,128)(2,1)} %build.1), calls=%async_computation | async-start | bytes 1048576 | tf_op jit(solution)/shard_map/all_to_all | solution.py:158
  20.0 14.4 %collective-permute-start.2 = (bf16[46,32,128]{2,1,0:T(8,128)(2,1)S(1)}, bf16[46,32,128]{2,1,0:T(8,128)(2,1)S(1)}, u32[]{:S(2)}, u32[]{:S(2)}) collective-permute-start(bf16[46,32,128]{2,1,0:T(8,128)(2,1)S(1)} %pad_maximum_fusion), channel_id=1, source_target_pairs={{0,0},{1,1},{2,6},{3,7},{4,4},{5,5},{6,2},{7,3},{8,8},{9,9},{10,14... | collective-permute-start | bytes 1130504 | tf_op jit(solution)/shard_map/ppermute | solution.py:167
  20.7 15.6 %collective-permute-start.3 = (bf16[45,32,128]{2,1,0:T(8,128)(2,1)S(1)}, bf16[45,32,128]{2,1,0:T(8,128)(2,1)S(1)}, u32[]{:S(2)}, u32[]{:S(2)}) collective-permute-start(bf16[45,32,128]{2,1,0:T(8,128)(2,1)S(1)} %bitcast.17), channel_id=1, source_target_pairs={{0,6},{1,7},{2,0},{3,1},{4,2},{5,3},{6,4},{7,5},{8,14},{9,15},{10,... | collective-permute-start | bytes 1105928 | tf_op jit(solution)/shard_map/ppermute | solution.py:167
  26.9 17.0 %collective-permute-start = (bf16[45,32,128]{2,1,0:T(8,128)(2,1)S(1)}, bf16[45,32,128]{2,1,0:T(8,128)(2,1)S(1)}, u32[]{:S(2)}, u32[]{:S(2)}) collective-permute-start(bf16[45,32,128]{2,1,0:T(8,128)(2,1)S(1)} %bitcast.18), channel_id=1, source_target_pairs={{0,1},{1,6},{2,7},{3,0},{4,5},{5,2},{6,3},{7,4},{8,9},{9,14},{10,1... | collective-permute-start | bytes 1105928 | tf_op jit(solution)/shard_map/ppermute | solution.py:167
  29.5 14.7 %collective-permute-start.1 = (bf16[45,32,128]{2,1,0:T(8,128)(2,1)S(1)}, bf16[45,32,128]{2,1,0:T(8,128)(2,1)S(1)}, u32[]{:S(2)}, u32[]{:S(2)}) collective-permute-start(bf16[45,32,128]{2,1,0:T(8,128)(2,1)S(1)} %bitcast.19), channel_id=1, source_target_pairs={{0,7},{1,0},{2,1},{3,6},{4,3},{5,4},{6,5},{7,2},{8,15},{9,8},{10,9... | collective-permute-start | bytes 1105928 | tf_op jit(solution)/shard_map/ppermute | solution.py:167
  33.4 0.7 copy-start.1

commit v4 on v3

--- a/solution.py
+++ b/solution.py
@@ -50,21 +50,39 @@
         out_ref[place] = query_ref[table[chip * CORES + owner_core]]
 
 
+def fill_slices(part_refs, ends_ref, token_ref, shifts, parts):
+    length = token_ref.shape[1]
+    ends = ends_ref[0].astype(jnp.float32)
+    plane = lax.axis_index("tok")
+    for place, shift in enumerate(shifts):
+        start = ((plane - shift + parts) % parts * length).astype(jnp.float32)
+        left = (ends - start).astype(token_ref.dtype)
+        first = part_refs[place][0]
+        for j in range(length):
+            token_ref[place, j] = jnp.where(left > j, part_refs[place][j], first)
+
+
+def fill_kernel(*refs, shifts, parts):
+    *part_refs, ends_ref, token_ref = refs
+    fill_slices(part_refs, ends_ref, token_ref, shifts, parts)
+
+
 def best_kernel(*refs, shifts, parts, tile, query_len, last):
-    *given_refs, ends_ref, query_ref, out_ref, token_ref = refs
-    part_refs, before_refs = given_refs[: len(shifts)], given_refs[len(shifts) :]
+    if last:
+        *part_refs, before_ref, ends_ref, query_ref, out_ref, token_ref = refs
+        before_refs = [before_ref]
+        fill_slices(part_refs, ends_ref, token_ref, shifts, parts)
+    else:
+        token_ref, ends_ref, query_ref, out_ref = refs
+        before_refs = []
     length, width, dim = token_ref.shape[1:]
     items = tile // query_len
     plane = lax.axis_index("tok")
     ends = ends_ref[0].astype(jnp.float32)
     used = []
-    for place, shift in enumerate(shifts):
+    for shift in shifts:
         start = ((plane - shift + parts) % parts * length).astype(jnp.float32)
         used.append(jnp.concatenate([ends > start] * (tile // LANES), axis=1))
-        left = (ends - start).astype(token_ref.dtype)
-        first = part_refs[place][0]
-        for j in range(length):
-            token_ref[place, j] = jnp.where(left > j, part_refs[place][j], first)
 
     def one_tile(index, carry):
         rows = query_ref[pl.ds(pl.multiple_of(index * tile, tile), tile), :]
@@ -182,13 +200,25 @@
         kernel = functools.partial(
             best_kernel, shifts=shifts, parts=num_parts, tile=TILE, query_len=query_len, last=last
         )
-        inputs = [parts[shift] for shift in shifts] + ([maxima] if last else []) + [ends, rows]
+        slices = [parts[shift] for shift in shifts]
+        shape = (len(shifts), local_len, pass_width, dim_width)
+        if last:
+            inputs = slices + [maxima, ends, rows]
+        else:
+            filled = pl.pallas_call(
+                functools.partial(fill_kernel, shifts=shifts, parts=num_parts),
+                out_shape=pltpu.VMEM(shape, own.dtype),
+                in_specs=[VMEM] * (len(slices) + 1),
+                out_specs=VMEM,
+                name="fill",
+            )(*near(*slices, ends))
+            inputs = [filled, ends, rows]
         maxima = pl.pallas_call(
             kernel,
             out_shape=pltpu.VMEM(whole, jnp.float32),
             in_specs=[VMEM] * len(inputs),
             out_specs=VMEM,
-            scratch_shapes=[pltpu.VMEM((len(shifts), local_len, pass_width, dim_width), own.dtype)],
+            scratch_shapes=[pltpu.VMEM(shape, own.dtype)] if last else [],
             name="best",
         )(*near(*inputs))
     totals = maxima

time: 74.9 us -> 75.9 us (1.013)
  other arithmetic: 0.16 us -> 1.15 us
    concatenate x1, other arithmetic: 0.03 us -> 1.02 us  [shards(): payload = own if shift else jnp.concatenate([own, ends])]
  transfers between devices with their start and end apart: 5 -> 5, of which waited for: 3 -> 3; matrix products, arithmetic and copies ran while one was open for 1% -> 2% of each run, Pallas kernels for 4% -> 4%
where the time goes in v4:
time: 75.9 us; the launch traced here: 75.5 us
  starting transfers between devices  31.2 us (41%)
  blocking collectives  26 us (34%)
  Pallas kernels  9.44 us (12%)
  waiting for transfers between devices  6.66 us (9%)
  other arithmetic  1.15 us (2%)
  local copies, waits for them, and re-layouts  0.92 us (1%)
    all_to_all x1, starting transfers between devices, shards(): lax.all_to_all(outgoing, 'blk', split_axis=0, concat_axis=0, axis_index_g...  17.9 us
    all_to_all x1, blocking collectives, shards(): lax.all_to_all(totals.reshape(chips, 1, pass_width), 'blk', split_axis=0,...  16.7 us
    ppermute x4, starting transfers between devices, shards(): parts.append(lax.ppermute(payload, ('blk', 'tok'), pairs))  13.4 us
    all_to_all x1, blocking collectives, shards(): lax.all_to_all(spread, 'tok', split_axis=0, concat_axis=0, tiled=True)  9.31 us
    ppermute x4, waiting for transfers between devices, shards(): parts.append(lax.ppermute(payload, ('blk', 'tok'), pairs))  6.65 us
    pallas_call x2, Pallas kernels, shards(): pl.pallas_call(kernel, out_shape=pltpu.VMEM(whole, jnp.float32), in_specs...  6.62 us
    pallas_call x1, Pallas kernels, shards(): outgoing = build(turned, queries)  1.81 us
  transfers between devices with their start and end apart: 5, of which 3 were waited for; matrix products, arithmetic and copies ran while one was open for 2% of the time, Pallas kernels for 4%

profile of v4, /device:TPU:8, one launch (start us, length us, event | category | flops | bytes accessed | tf_op | source)
XLA Modules:
  0.0 75.5 jit_solution(8988235612831825023)
XLA Ops:
  0.0 1.8 %build.1 = bf16[64,32,128]{2,1,0:T(8,128)(2,1)} custom-call(s32[4,32]{1,0:T(4,128)} %bitcast.16, bf16[32,32,128]{2,1,0:T(8,128)(2,1)} %query_hbm.1), custom_call_target="tpu_custom_call" | custom-call | tf_op jit(solution)/shard_map/build/pallas_call | solution.py:175
  1.8 0.0 copy-start.1
  1.8 17.9 %all-to-all-start = ((bf16[64,32,128]{2,1,0:T(8,128)(2,1)}), bf16[64,32,128]{2,1,0:T(8,128)(2,1)S(1)}, u32[]{:S(2)}, u32[]{:S(2)}) async-start(bf16[64,32,128]{2,1,0:T(8,128)(2,1)} %build.1), calls=%async_computation | async-start | bytes 1048576 | tf_op jit(solution)/shard_map/all_to_all | solution.py:176
  19.7 0.0 copy-done.1
  19.7 0.1 broadcast_in_dim.2
  19.8 1.0 %pad_maximum_fusion = bf16[46,32,128]{2,1,0:T(8,128)(2,1)S(1)} fusion(bf16[1,32,128]{2,1,0:T(8,128)(2,1)S(1)} %broadcast_in_dim.2, bf16[45,32,128]{2,1,0:T(8,128)(2,1)} %bitcast), kind=kLoop, calls=%fused_computation | loop fusion | flops 188416 | bytes 753664 | tf_op jit(solution)/shard_map/concatenate | solution.py:184
  20.8 0.7 collective-permute-start.2
  21.5 6.3 %collective-permute-start.3 = (bf16[45,32,128]{2,1,0:T(8,128)(2,1)}, bf16[45,32,128]{2,1,0:T(8,128)(2,1)S(1)}, u32[]{:S(2)}, u32[]{:S(2)}) collective-permute-start(bf16[45,32,128]{2,1,0:T(8,128)(2,1)} %bitcast), channel_id=1, source_target_pairs={{0,6},{1,7},{2,0},{3,1},{4,2},{5,3},{6,4},{7,5},{8,14},{9,15},{10,... | collective-permute-start | bytes 1105928 | tf_op jit(solution)/shard_map/ppermute | solution.py:185
  27.8 2.5 %collective-permute-start = (bf16[45,32,128]{2,1,0:T(8,128)(2,1)}, bf16[45,32,128]{2,1,0:T(8,128)(2,1)S(1)}, u32[]{:S(2)}, u32[]{:S(2)}) collective-permute-start(bf16[45,32,128]{2,1,0:T(8,128)(2,1)} %bitcast), channel_id=1, source_target_pairs={{0,1},{1,6},{2,7},{3,0},{4,5},{5,2},{6,3},{7,4},{8,9},{9,14},{10,1... | collective-permute-start | bytes 1105928 | tf_op jit(solution)/shard_map/ppermute | solution.py:185
  30.3 3.9 %collective-permute-start.1 = (bf16[45,32,128]{2,1,0:T(8,128)(2,1)}, bf16[45,32,128]{2,1,0:T(8,128)(2,1)S(1)}, u32[]{:S(2)}, u32[]{:S(2)}) collective-permute-start(bf16[45,32,128]{2,1,0:T(8,128)(2,1)} %bitcast), channel_id=1, source_target_pairs={{0,7},{1,0},{2,1},{3,6},{4,3},{5,4},{6,5},{7,2},{8,15},{9,8},{10,9... | collective-permute-start | bytes 1105928 | tf_op jit(solution)/shard_map/ppermute | solution.py:185
  34.2 0.0 copy-start
  34.2 0.7 copy-done
  34.9 0.1 eq.20
  35.0 0.1 reshape.172
  35.1 0.1 convert_reduce_fusion
  35.2 0.0 collective-permute-done.2.refs_0_
  35.2 2.2 %collective-permute-done.3.refs_1_ = bf16[45,32,128]{2,1,0:T(8,128)(2,1)S(1)} collective-permute-done((bf16[45,32,128]{2,1,0:T(8,128)(2,1)}, bf16[45,32,128]{2,1,0:T(8,128)(2,1)S(1)}, u32[]{:S(2)}, u32[]{:S(2)}) %collective-permute-start.3) | collective-permute-done | bytes 368672 | tf_op jit(solution)/shard_map/ppermute | solution.py:185
  37.4 0.1 fill.1.refs_0_
  37.5 0.0 all-to-all-done
  37.5 3.2 %best.2.refs_2_ = f32[1,32,2048]{2,1,0:T(8,128)S(1)} custom-call(bf16[2,45,32,128]{3,2,1,0:T(8,128)(2,1)S(1)} %fill.1.refs_0_, bf16[1,32,128]{2,1,0:T(8,128)(2,1)S(1)} %slice.4.refs_2_.refs_1_.refs_3_, bf16[2048,128]{1,0:T(8,128)(2,1)S(1)} %bitcast.12), custom_call_target="tpu_custom_call" | custom-call | tf_op jit(solution)/shard_map/best/pallas_call | solution.py:216
  40.7 4.3 %collective-permute-done.refs_0_ = bf16[45,32,128]{2,1,0:T(8,128)(2,1)S(1)} collective-permute-done((bf16[45,32,128]{2,1,0:T(8,128)(2,1)}, bf16[45,32,128]{2,1,0:T(8,128)(2,1)S(1)}, u32[]{:S(2)}, u32[]{:S(2)}) %collective-permute-start) | collective-permute-done | bytes 368672 | tf_op jit(solution)/shard_map/ppermute | solution.py:185
  45.0 0.2 collective-permute-done.1.refs_1_
  45.2 3.4 %best.3 = f32[64,32]{1,0:T(8,128)S(1)} custom-call(bf16[45,32,128]{2,1,0:T(8,128)(2,1)S(1)} %collective-permute-done.refs_0_, bf16[45,32,128]{2,1,0:T(8,128)(2,1)S(1)} %collective-permute-done.1.refs_1_, f32[1,32,2048]{2,1,0:T(8,128)S(1)} %best.2.refs_2_, bf16[1,32,128]{2,1,0:T(8,128)(2,1)S(1)} %slice.4.refs_2_.refs_1_.refs_3_, bf16[2048,128]{1,0:T(8,128)(2,1)S(1)} %bitcast.13), custom_call_target="tpu_custom_call" | custom-call | tf_op jit(solution)/shard_map/best/pallas_call | solution.py:216
  48.6 16.7 %all_to_all.15 = f32[64,1,32]{2,1,0:T(1,128)S(1)} all-to-all(f32[64,1,32]{2,1,0:T(1,128)S(1)} %bitcast.14), channel_id=1, replica_groups={{352,360,368,376,384,392,400,408,416,424,432,440,448,456,464,472,480,48..., dimensions={0} | all-to-all | bytes 16384 | tf_op jit(solution)/shard_map/all_to_all | solution.py:226
  65.3 0.1 turn.1
  65.4 9.3 %all_to_all.16.in_ref = f32[4,8,128]{2,1,0:T(8,128)S(1)} all-to-all(f32[4,8,128]{2,1,0:T(8,128)S(1)} %turn.1), channel_id=1, replica_groups=mesh['blk'=128,'tok'=4] {'tok'}, dimensions={0} | all-to-all | bytes 32768 | tf_op jit(solution)/shard_map/all_to_all | solution.py:237
  74.7 0.8 pick.1
  (3 shorter events, 0.0 us)
Async XLA Ops:
  1.8 17.9 %copy-start.1 = (s32[1,32]{1,0:T(1,128)S(1)}, s32[1,32]{1,0:T(1,128)}, u32[]{:S(2)}) copy-start(s32[1,32]{1,0:T(1,128)} %param.7) | copy-start | bytes 388
  1.8 35.7 %all-to-all-start = ((bf16[64,32,128]{2,1,0:T(8,128)(2,1)}), bf16[64,32,128]{2,1,0:T(8,128)(2,1)S(1)}, u32[]{:S(2)}, u32[]{:S(2)}) async-start(bf16[64,32,128]{2,1,0:T(8,128)(2,1)} %build.1), calls=%async_computation | async-start | bytes 1048576 | tf_op jit(solution)/shard_map/all_to_all | solution.py:176
  20.8 14.4 %collective-permute-start.2 = (bf16[46,32,128]{2,1,0:T(8,128)(2,1)S(1)}, bf16[46,32,128]{2,1,0:T(8,128)(2,1)S(1)}, u32[]{:S(2)}, u32[]{:S(2)}) collective-permute-start(bf16[46,32,128]{2,1,0:T(8,128)(2,1)S(1)} %pad_maximum_fusion), channel_id=1, source_target_pairs={{0,0},{1,1},{2,6},{3,7},{4,4},{5,5},{6,2},{7,3},{8,8},{9,9},{10,14... | collective-permute-start | bytes 1130504 | tf_op jit(solution)/shard_map/ppermute | solution.py:185
  21.5 15.9 %collective-permute-start.3 = (bf16[45,32,128]{2,1,0:T(8,128)(2,1)}, bf16[45,32,128]{2,1,0:T(8,128)(2,1)S(1)}, u32[]{:S(2)}, u32[]{:S(2)}) collective-permute-start(bf16[45,32,128]{2,1,0:T(8,128)(2,1)} %bitcast), channel_id=1, source_target_pairs={{0,6},{1,7},{2,0},{3,1},{4,2},{5,3},{6,4},{7,5},{8,14},{9,15},{10,... | collective-permute-start | bytes 1105928 | tf_op jit(solution)/shard_map/ppermute | solution.py:185
  27.8 17.2 %collective-permute-start = (bf16[45,32,128]{2,1,0:T(8,128)(2,1)}, bf16[45,32,128]{2,1,0:T(8,128)(2,1)S(1)}, u32[]{:S(2)}, u32[]{:S(2)}) collective-permute-start(bf16[45,32,128]{2,1,0:T(8,128)(2,1)} %bitcast), channel_id=1, source_target_pairs={{0,1},{1,6},{2,7},{3,0},{4,5},{5,2},{6,3},{7,4},{8,9},{9,14},{10,1... | collective-permute-start | bytes 1105928 | tf_op jit(solution)/shard_map/ppermute | solution.py:185
  30.3 14.9 %collective-permute-start.1 = (bf16[45,32,128]{2,1,0:T(8,128)(2,1)}, bf16[45,32,128]{2,1,0:T(8,128)(2,1)S(1)}, u32[]{:S(2)}, u32[]{:S(2)}) collective-permute-start(bf16[45,32,128]{2,1,0:T(8,128)(2,1)} %bitcast), channel_id=1, source_target_pairs={{0,7},{1,0},{2,1},{3,6},{4,3},{5,4},{6,5},{7,2},{8,15},{9,8},{10,9... | collective-permute-start | bytes 1105928 | tf_op jit(solution)/shard_map/ppermute | solution.py:185
  34.2 0.7 copy-start
